TPU v7x, 256 devices: a whole 4x4x8 slice. The times are simulated.
256 devices in a mesh: row: 32 (over x, z_hi, core), col: 8 (over y, z_lo).
Axes of the slice: x: 4, y: 4, z: 8 (z_hi: 4, z_lo: 2; z = z_hi * 2 + z_lo), core: 2. Of those that a mesh axis runs over, the one named last changes fastest.
Arguments:
- ancestor_inverse: bfloat16 [24576, 8, 3072], P('row', 'col'), may hold values from -6 to 6
- parent_panel: bfloat16 [24576, 1024], P(('row', 'col')), may hold values from -0.15625 to 0.15625
- parent_diag_inv: bfloat16 [1024, 1024], replicated, may hold values from -1.5 to 1.5, as said below
- child_panel_anc: bfloat16 [24576, 1024], P(('row', 'col')), may hold values from -0.15625 to 0.15625
- child_panel_par: bfloat16 [1024, 1024], replicated, may hold values from -0.1875 to 0.1875
- child_diag_inv: bfloat16 [1024, 1024], replicated, may hold values from -1.5 to 1.5, as said below
Outputs:
- ainv_ap: float32 [24576, 1024], P(('row', 'col'))
- ainv_pp: float32 [1024, 1024], P(('row', 'col'))
- ainv_ac: float32 [24576, 1024], P(('row', 'col'))
- ainv_pc: float32 [1024, 1024], P(('row', 'col'))
- ainv_cc: float32 [1024, 1024], P(('row', 'col'))
Inputs may be any that keep to these rules, and one draw needn't show every extreme that they name: `parent_diag_inv`: lower triangular, with diagonal entries between 0.5 and 1.5. `child_diag_inv`: lower triangular, with diagonal entries between 0.5 and 1.5.
All inputs are finite; a program needn't handle non-finite values.
Results may differ from a plain program's by a relative error of at most 0.0041.
Values may be sent and summed in bfloat16 or wider, within the bound.
No kernel may reach another device: no remote copies, remote signals or barrier semaphores. Data moves between devices by JAX's collectives and lax.ppermute only.
A program may use at most 128 MiB of HBM per device.

v0:
```python
import jax
import jax.numpy as jnp
from jax import lax
from jax.sharding import PartitionSpec as P


def contract_rows(left_side, right_side):
    return lax.dot_general(
        left_side, right_side, (((0,), (0,)), ((), ())), preferred_element_type=jnp.float32
    )


def shards(
    ancestor_inverse,
    parent_panel,
    parent_diag_inv,
    child_panel_anc,
    child_panel_par,
    child_diag_inv,
):
    local_rows = ancestor_inverse.shape[0]
    local_block = ancestor_inverse.reshape(local_rows, -1)
    columns = parent_panel.shape[1]

    def add_panel(pieces):
        return jnp.dot(local_block, pieces, preferred_element_type=jnp.float32)

    pieces = (
        lax.all_gather(parent_panel, "row", axis=0, tiled=True),
        lax.all_gather(child_panel_anc, "row", axis=0, tiled=True),
    )
    partial_upper = add_panel(pieces[0])
    partial_lower = add_panel(pieces[1])
    upper_prod, lower_first = (
        lax.psum_scatter(partial_upper, "col", scatter_dimension=0, tiled=True),
        lax.psum_scatter(partial_lower, "col", scatter_dimension=0, tiled=True),
    )
    upper_round = upper_prod.astype(jnp.bfloat16)
    shifted = jnp.dot(upper_round, child_panel_par, preferred_element_type=jnp.float32)
    shifted_round = shifted.astype(jnp.bfloat16)
    lower_prod_anc = lower_first - shifted
    anc_round = lower_prod_anc.astype(jnp.bfloat16)
    mixed_round = jnp.dot(parent_panel, child_panel_par, preferred_element_type=jnp.float32).astype(
        jnp.bfloat16
    )
    diag_prod = jnp.dot(
        parent_diag_inv, child_panel_par, preferred_element_type=jnp.float32
    ).astype(jnp.bfloat16)
    devices = lax.axis_size("row") * lax.axis_size("col")
    my_rows = columns // devices
    position = lax.axis_index("row") * lax.axis_size("col") + lax.axis_index("col")
    first_row = position * my_rows
    parent_cols = lax.dynamic_slice_in_dim(parent_diag_inv, first_row, my_rows, 1)
    diag_upper = contract_rows(parent_cols, parent_diag_inv)
    child_cols = lax.dynamic_slice_in_dim(child_diag_inv, first_row, my_rows, 1)
    prod_cols = lax.dynamic_slice_in_dim(diag_prod, first_row, my_rows, 1)
    diag_lower = contract_rows(child_cols, child_diag_inv) + contract_rows(prod_cols, diag_prod)
    from_anc = contract_rows(child_panel_anc, anc_round)
    from_mixed = contract_rows(mixed_round, shifted_round)
    from_shift = contract_rows(shifted_round, child_panel_anc)
    joined_sum = lax.psum_scatter(
        jnp.concatenate(
            [
                contract_rows(parent_panel, upper_round),
                contract_rows(upper_round, child_panel_anc),
                from_anc + from_mixed - from_shift,
            ],
            axis=1,
        ),
        ("row", "col"),
        scatter_dimension=0,
        tiled=True,
    )
    upper_sum = joined_sum[:, :columns]
    cross_sum = joined_sum[:, columns : 2 * columns]
    lower_sum = joined_sum[:, 2 * columns :]
    ainv_pp = diag_upper + upper_sum
    pp_round = ainv_pp.astype(jnp.bfloat16)
    lower_prod_par = (
        jnp.dot(pp_round, child_panel_par, preferred_element_type=jnp.float32) - cross_sum
    )
    ainv_cc = diag_lower + lower_sum
    return (-upper_prod, ainv_pp, -lower_prod_anc, -lower_prod_par, ainv_cc)


def solution(mesh):
    placed = (
        P("row", "col", None),
        P(("row", "col"), None),
        P(),
        P(("row", "col"), None),
        P(),
        P(),
    )
    return jax.shard_map(
        shards,
        mesh=mesh,
        in_specs=placed,
        out_specs=(
            P(("row", "col"), None),
            P(("row", "col"), None),
            P(("row", "col"), None),
            P(("row", "col"), None),
            P(("row", "col"), None),
        ),
        check_vma=False,
    )
```

profile of v0, /device:TPU:8, one launch (start us, length us, event | category | flops | bytes accessed | tf_op | source)
XLA Modules:
  0.0 634.1 jit_solution(10543304892223463329)
XLA Ops:
  8.0 0.7 all-gather.5.cloned.1.call-update
  8.7 73.7 %all-gather.3.cloned.1.call-done = bf16[3072,1024]{1,0:T(8,128)(2,1)} async-done(((bf16[96,1024]{1,0:T(8,128)(2,1)}), bf16[3072,1024]{1,0:T(8,128)(2,1)}) %all-gather.3.cloned.1.call-update) | async-done | bytes 6291472 | tf_op jit(solution)/shard_map/all_gather | solution.py:29
  82.4 9.7 %fusion.2 = f32[768,1024]{1,0:T(8,128)} fusion(bf16[3072,1024]{1,0:T(8,128)(2,1)} %all-gather.3.cloned.1.call-done, bf16[768,1,3072]{2,0,1:T(8,128)(2,1)} %param.6), kind=kOutput, calls=%fused_computation.3 | convolution fusion | flops 4831838208 | bytes 14155776 | tf_op jit(solution)/shard_map/dot_general | solution.py:26
  92.2 59.7 %all-gather.5.cloned.1.call-done = bf16[3072,1024]{1,0:T(8,128)(2,1)} async-done(((bf16[96,1024]{1,0:T(8,128)(2,1)}), bf16[3072,1024]{1,0:T(8,128)(2,1)}) %all-gather.5.cloned.1.call-update) | async-done | bytes 6291472 | tf_op jit(solution)/shard_map/all_gather | solution.py:30
  151.9 9.7 %fusion = f32[768,1024]{1,0:T(8,128)} fusion(bf16[3072,1024]{1,0:T(8,128)(2,1)} %all-gather.5.cloned.1.call-done, bf16[768,1,3072]{2,0,1:T(8,128)(2,1)} %param.6), kind=kOutput, calls=%fused_computation.1 | convolution fusion | flops 4831838208 | bytes 14155776 | tf_op jit(solution)/shard_map/dot_general | solution.py:26
  161.9 63.8 %reduce-scatter.3.cloned.1.call-done = f32[96,1024]{1,0:T(8,128)} async-done(((f32[768,1024]{1,0:T(8,128)}), f32[96,1024]{1,0:T(8,128)}) %reduce-scatter.3.cloned.1.call-update) | async-done | bytes 393232 | tf_op jit(solution)/shard_map/reduce_scatter | solution.py:35
  225.7 76.5 %reduce-scatter.5.cloned.1.call-done = f32[96,1024]{1,0:T(8,128)} async-done(((f32[768,1024]{1,0:T(8,128)}), f32[96,1024]{1,0:T(8,128)}) %reduce-scatter.5.cloned.1.call-update) | async-done | bytes 393232 | tf_op jit(solution)/shard_map/reduce_scatter | solution.py:36
  302.1 2.3 subtract_negate_fusion
  304.5 2.7 fusion.13
  307.2 3.0 fusion.5
  310.2 0.7 convolution_bitcast_fusion
  311.0 0.8 fusion.23
  311.7 0.7 copy-done.1
  312.4 1.3 copy-done.2
  313.7 0.9 fusion.4
  314.6 5.6 pad_maximum_fusion
  320.2 12.6 %copy.16 = f32[1024,3072]{1,0:T(8,128)} copy(f32[1024,3072]{0,1:T(8,128)} %pad_maximum_fusion) | data formatting | bytes 25165824 | tf_op jit(solution)/shard_map/concatenate | solution.py:62
  332.9 2.2 fusion.8
  335.0 5.4 convolution_convert_fusion
  340.4 0.8 neg.9
  341.2 280.3 %all-reduce.3.cloned.1.call-done = f32[1024,3072]{1,0:T(8,128)} async-done(((f32[1024,3072]{1,0:T(8,128)}), f32[1024,3072]{1,0:T(8,128)}) %all-reduce.3.cloned.1.call-update) | async-done | bytes 12582928
  621.5 2.2 convolution_add_fusion.1
  623.7 1.8 fusion.7
  625.5 2.0 fusion.6
  (25 shorter events, 1.1 us)
Async XLA Ops:
  7.2 295.0 %copy-start = (bf16[1024,1024]{1,0:T(8,128)(2,1)S(1)}, bf16[1024,1024]{1,0:T(8,128)(2,1)}, u32[]{:S(2)}) copy-start(bf16[1024,1024]{1,0:T(8,128)(2,1)} %param.10) | copy-start | bytes 6291460
  7.2 75.2 %all-gather.3.cloned.1.call-start = ((), (), s32[]{:S(2)}) async-start(), calls=%async_computation.2 | async-start | bytes 6488064 | tf_op jit(solution)/shard_map/all_gather | solution.py:29
  7.9 144.0 %all-gather.5.cloned.1.call-start = ((), (), s32[]{:S(2)}) async-start(), calls=%async_computation.4 | async-start | bytes 6488064 | tf_op jit(solution)/shard_map/all_gather | solution.py:30
  8.7 217.0 %reduce-scatter.3.cloned.1.call-start = ((), (), s32[]{:S(2)}) async-start(), calls=%async_computation.3 | async-start | bytes 3538944 | tf_op jit(solution)/shard_map/reduce_scatter | solution.py:35
  92.1 210.0 %reduce-scatter.5.cloned.1.call-start = ((), (), s32[]{:S(2)}) async-start(), calls=%async_computation.5 | async-start | bytes 3538944 | tf_op jit(solution)/shard_map/reduce_scatter | solution.py:36
  161.6 142.9 %copy-start.4 = (bf16[96,1024]{1,0:T(8,128)(2,1)S(1)}, bf16[96,1024]{1,0:T(8,128)(2,1)}, u32[]{:S(2)}) copy-start(bf16[96,1024]{1,0:T(8,128)(2,1)} %param.9) | copy-start | bytes 589828
  161.6 145.6 %copy-start.6 = (bf16[96,1024]{1,0:T(8,128)(2,1)S(1)}, bf16[96,1024]{1,0:T(8,128)(2,1)}, u32[]{:S(2)}) copy-start(bf16[96,1024]{1,0:T(8,128)(2,1)} %param.7) | copy-start | bytes 589828
  161.6 459.9 %all-reduce.3.cloned.1.call-start = ((), (), s32[]{:S(2)}) async-start(), calls=%async_computation.6 | async-start | bytes 25165824
  307.2 3.0 copy-start.3
  310.2 2.2 copy-start.1
  310.2 3.5 copy-start.2
  310.2 3.5 copy-start.7
  621.5 4.0 copy-start.5
  623.7 3.8 copy-start.8
Sparse Core Ops, SparseCore 0:
  10.6 71.7 all-gather.2
  84.9 66.9 all-gather.4
  154.5 71.1 reduce-scatter.2
  228.1 74.0 reduce-scatter.4
  333.0 288.4 all-reduce.2
where the time goes:
time: 635 us; the launch traced here: 634 us
  waiting for transfers between devices  555 us (87%)
  matrix products  43.4 us (7%)
  local copies, waits for them, and re-layouts  14.6 us (2%)
  between operations  13.8 us (2%)
  other arithmetic  6.41 us (1%)
    unnamed x6, waiting for transfers between devices  282 us
    reduce_scatter x1, waiting for transfers between devices, shards(): lax.psum_scatter(partial_lower, 'col', scatter_dimension=0, tiled=True)  76.5 us
    all_gather x1, waiting for transfers between devices, shards(): lax.all_gather(parent_panel, 'row', axis=0, tiled=True)  73.7 us
    reduce_scatter x1, waiting for transfers between devices, shards(): lax.psum_scatter(partial_upper, 'col', scatter_dimension=0, tiled=True)  63.8 us
    all_gather x1, waiting for transfers between devices, shards(): lax.all_gather(child_panel_anc, 'row', axis=0, tiled=True)  59.7 us
    dot_general x2, matrix products, add_panel(): return jnp.dot(local_block, pieces, preferred_element_type=jnp.float32)  19.4 us
    dot_general x8, matrix products, contract_rows(): lax.dot_general(left_side, right_side, (((0,), (0,)), ((), ())), preferre...  14.5 us
  transfers between devices with their start and end apart: 5, of which 5 were waited for; matrix products, arithmetic and copies ran while one was open for 4% of the time, Pallas kernels for 0%

commit v1 on v0

--- a/solution.py
+++ b/solution.py
@@ -1,7 +1,18 @@
+import functools
 import jax
 import jax.numpy as jnp
 from jax import lax
 from jax.sharding import PartitionSpec as P
+
+
+def carry_tables(mat, a_name):
+    return jnp.concatenate(
+        lax.all_to_all(jnp.stack(tuple((mat for _ in range(lax.axis_size(a_name))))), a_name, 0, 0),
+        axis=0,
+    )
+
+
+orders_lift = functools.partial(carry_tables, a_name="row")
 
 
 def contract_rows(left_side, right_side):
@@ -25,10 +36,7 @@
     def add_panel(pieces):
         return jnp.dot(local_block, pieces, preferred_element_type=jnp.float32)
 
-    pieces = (
-        lax.all_gather(parent_panel, "row", axis=0, tiled=True),
-        lax.all_gather(child_panel_anc, "row", axis=0, tiled=True),
-    )
+    pieces = (lax.all_gather(parent_panel, "row", axis=0, tiled=True), orders_lift(child_panel_anc))
     partial_upper = add_panel(pieces[0])
     partial_lower = add_panel(pieces[1])
     upper_prod, lower_first = (

time: 635 us -> 672 us (1.058)
  waiting for transfers between devices: 555 us -> 578 us
  starting transfers between devices: 0.38 us -> 11.8 us
    all_gather x1, waiting for transfers between devices: 73.7 us -> 155 us  [shards(): lax.all_gather(parent_panel, 'row', axis=0, tiled=True)]
    all_gather x1 -> x0, waiting for transfers between devices: 59.7 us -> none  [shards(): lax.all_gather(child_panel_anc, 'row', axis=0, tiled=True)]
    all_to_all x0 -> x1, starting transfers between devices: none -> 11.4 us  [carry_tables(): lax.all_to_all(jnp.stack(tuple((mat for _ in range(lax.axis_size(a_name))...]
    unnamed x6 -> x5, waiting for transfers between devices: 282 us -> 282 us
  transfers between devices with their start and end apart: 5 -> 5, of which waited for: 5 -> 5; matrix products, arithmetic and copies ran while one was open for 4% -> 5% of each run, Pallas kernels for 0% -> 0%
where the time goes in v1:
time: 672 us
  waiting for transfers between devices  578 us (86%)
  matrix products  43.4 us (6%)
  local copies, waits for them, and re-layouts  19 us (3%)
  between operations  13.8 us (2%)
  starting transfers between devices  11.8 us (2%)
    unnamed x5, waiting for transfers between devices  282 us
    all_gather x1, waiting for transfers between devices, shards(): lax.all_gather(parent_panel, 'row', axis=0, tiled=True)  155 us
    reduce_scatter x1, waiting for transfers between devices, shards(): lax.psum_scatter(partial_lower, 'col', scatter_dimension=0, tiled=True)  76.6 us
    reduce_scatter x1, waiting for transfers between devices, shards(): lax.psum_scatter(partial_upper, 'col', scatter_dimension=0, tiled=True)  58.5 us
    dot_general x2, matrix products, add_panel(): return jnp.dot(local_block, pieces, preferred_element_type=jnp.float32)  19.4 us
    dot_general x8, matrix products, contract_rows(): lax.dot_general(left_side, right_side, (((0,), (0,)), ((), ())), preferre...  14.5 us
  transfers between devices with their start and end apart: 5, of which 5 were waited for; matrix products, arithmetic and copies ran while one was open for 5% of the time, Pallas kernels for 0%

profile of v1, /device:TPU:8, one launch (start us, length us, event | category | flops | bytes accessed | tf_op | source)
XLA Modules:
  0.0 671.9 jit_solution(17013988099500970660)
XLA Ops:
  7.9 4.4 stack.2
  12.3 11.4 %all-to-all-start = ((bf16[32,96,1024]{2,1,0:T(8,128)(2,1)}), bf16[32,96,1024]{2,1,0:T(8,128)(2,1)}, u32[]{:S(2)}, u32[]{:S(2)}) async-start(bf16[32,96,1024]{2,1,0:T(8,128)(2,1)} %stack.2), calls=%async_computation.1 | async-start | bytes 12582912 | tf_op jit(solution)/shard_map/all_to_all | solution.py:10
  23.8 155.4 %all-gather.2.cloned.1.call-done = bf16[3072,1024]{1,0:T(8,128)(2,1)} async-done(((bf16[96,1024]{1,0:T(8,128)(2,1)}), bf16[3072,1024]{1,0:T(8,128)(2,1)}) %all-gather.2.cloned.1.call-update) | async-done | bytes 6291472 | tf_op jit(solution)/shard_map/all_gather | solution.py:39
  179.1 9.7 %fusion.2 = f32[768,1024]{1,0:T(8,128)} fusion(bf16[3072,1024]{1,0:T(8,128)(2,1)} %all-gather.2.cloned.1.call-done, bf16[768,1,3072]{2,0,1:T(8,128)(2,1)} %param.6), kind=kOutput, calls=%fused_computation.3 | convolution fusion | flops 4831838208 | bytes 14155776 | tf_op jit(solution)/shard_map/dot_general | solution.py:37
  188.9 5.4 all-to-all-done
  194.4 9.7 %fusion = f32[768,1024]{1,0:T(8,128)} fusion(bf16[3072,1024]{1,0:T(8,128)(2,1)} %bitcast.2, bf16[768,1,3072]{2,0,1:T(8,128)(2,1)} %param.6), kind=kOutput, calls=%fused_computation.1 | convolution fusion | flops 4831838208 | bytes 14155776 | tf_op jit(solution)/shard_map/dot_general | solution.py:37
  204.3 58.5 %reduce-scatter.3.cloned.1.call-done = f32[96,1024]{1,0:T(8,128)} async-done(((f32[768,1024]{1,0:T(8,128)}), f32[96,1024]{1,0:T(8,128)}) %reduce-scatter.3.cloned.1.call-update) | async-done | bytes 393232 | tf_op jit(solution)/shard_map/reduce_scatter | solution.py:43
  262.9 76.6 %reduce-scatter.5.cloned.1.call-done = f32[96,1024]{1,0:T(8,128)} async-done(((f32[768,1024]{1,0:T(8,128)}), f32[96,1024]{1,0:T(8,128)}) %reduce-scatter.5.cloned.1.call-update) | async-done | bytes 393232 | tf_op jit(solution)/shard_map/reduce_scatter | solution.py:44
  339.5 2.3 subtract_negate_fusion
  341.9 2.7 fusion.13
  344.6 3.0 fusion.5
  347.6 0.7 convolution_bitcast_fusion
  348.3 0.8 fusion.23
  349.8 1.3 copy-done.2
  351.1 0.9 fusion.4
  351.9 5.6 pad_maximum_fusion
  357.5 12.6 %copy.16 = f32[1024,3072]{1,0:T(8,128)} copy(f32[1024,3072]{0,1:T(8,128)} %pad_maximum_fusion) | data formatting | bytes 25165824 | tf_op jit(solution)/shard_map/concatenate | solution.py:70
  370.2 2.2 fusion.8
  372.3 5.4 convolution_convert_fusion
  377.7 0.8 neg.9
  378.5 280.9 %all-reduce.3.cloned.1.call-done = f32[1024,3072]{1,0:T(8,128)} async-done(((f32[1024,3072]{1,0:T(8,128)}), f32[1024,3072]{1,0:T(8,128)}) %all-reduce.3.cloned.1.call-update) | async-done | bytes 12582928
  659.4 2.2 convolution_add_fusion.1
  661.6 1.8 fusion.7
  663.4 2.0 fusion.6
  (25 shorter events, 1.8 us)
Async XLA Ops:
  7.2 332.4 %copy-start = (bf16[1024,1024]{1,0:T(8,128)(2,1)S(1)}, bf16[1024,1024]{1,0:T(8,128)(2,1)}, u32[]{:S(2)}) copy-start(bf16[1024,1024]{1,0:T(8,128)(2,1)} %param.10) | copy-start | bytes 6291460
  7.2 172.0 %all-gather.2.cloned.1.call-start = ((), (), s32[]{:S(2)}) async-start(), calls=%async_computation.3 | async-start | bytes 6488064 | tf_op jit(solution)/shard_map/all_gather | solution.py:39
  12.3 182.1 %all-to-all-start = ((bf16[32,96,1024]{2,1,0:T(8,128)(2,1)}), bf16[32,96,1024]{2,1,0:T(8,128)(2,1)}, u32[]{:S(2)}, u32[]{:S(2)}) async-start(bf16[32,96,1024]{2,1,0:T(8,128)(2,1)} %stack.2), calls=%async_computation.1 | async-start | bytes 12582912 | tf_op jit(solution)/shard_map/all_to_all | solution.py:10
  23.7 239.2 %reduce-scatter.3.cloned.1.call-start = ((), (), s32[]{:S(2)}) async-start(), calls=%async_computation.4 | async-start | bytes 3538944 | tf_op jit(solution)/shard_map/reduce_scatter | solution.py:43
  188.9 150.7 %reduce-scatter.5.cloned.1.call-start = ((), (), s32[]{:S(2)}) async-start(), calls=%async_computation.5 | async-start | bytes 3538944 | tf_op jit(solution)/shard_map/reduce_scatter | solution.py:44
  204.1 137.8 %copy-start.4 = (bf16[96,1024]{1,0:T(8,128)(2,1)S(1)}, bf16[96,1024]{1,0:T(8,128)(2,1)}, u32[]{:S(2)}) copy-start(bf16[96,1024]{1,0:T(8,128)(2,1)} %param.9) | copy-start | bytes 589828
  204.1 140.5 %copy-start.6 = (bf16[96,1024]{1,0:T(8,128)(2,1)S(1)}, bf16[96,1024]{1,0:T(8,128)(2,1)}, u32[]{:S(2)}) copy-start(bf16[96,1024]{1,0:T(8,128)(2,1)} %param.7) | copy-start | bytes 589828
  204.1 455.3 %all-reduce.3.cloned.1.call-start = ((), (), s32[]{:S(2)}) async-start(), calls=%async_computation.6 | async-start | bytes 25165824
  344.6 3.0 copy-start.3
  347.6 2.2 copy-start.1
  347.6 3.5 copy-start.2
  347.6 3.5 copy-start.7
  659.4 4.0 copy-start.5
  661.6 3.8 copy-start.8
Sparse Core Ops, SparseCore 0:
  10.6 168.5 all-gather.1
  189.0 73.8 reduce-scatter.2
  265.5 74.0 reduce-scatter.4
  370.3 289.0 all-reduce.2
